TPU v7x, 512 devices: a whole 4x8x8 slice. The times are simulated.
512 devices in a mesh: space: 256 (over z, y, x), sub: 2 (over core).
Axes of the slice: x: 4, y: 8, z: 8, core: 2. Of those that a mesh axis runs over, the one named last changes fastest.
Arguments:
- species: float32 [54, 1572864], P(None, ('space', 'sub')), may hold values from 0 to 1
- weight: float32 [1572864], P(('space', 'sub')), may hold values from 0.25 to 4
- destination: int32 [2, 1572864], P(None, ('space', 'sub')), may hold values from 0 to 511, as said below
- slot: int32 [2, 1572864], P(None, ('space', 'sub')), may hold values from 0 to 511, as said below
- counts: int32 [2, 3072], P(None, ('space', 'sub')), may hold values from 128 to 512, as said below
- cell_index: int32 [2, 1572864], P(None, ('space', 'sub')), may hold values from 0 to 511, as said below
- mix_rate: float32 [131072], P(('space', 'sub')), may hold values from 0.05 to 3
- rate_matrix: bfloat16 [54, 54], replicated, may hold values from -0.875 to 0.875
- rate_bias: float32 [54], replicated, may hold values from -1 to 1
Outputs:
- species_out: float32 [54, 1572864], P(None, ('space', 'sub'))
- weight_out: float32 [1572864], P(('space', 'sub'))
Inputs may be any that keep to these rules, and one draw needn't show every extreme that they name: `destination`: A slot of a device in slab a moves to a device of slab a - 1, a or a + 1, counted around the 256 slabs as a loop. Within one step, the slots of one device fill each of the six blocks to its six possible destinations completely, each block slot exactly once. `counts`: every device has in every step a block whose count is 512. `cell_index`: in every step each slab has at least 32 coarse cells to which exactly one particle slot belongs.
All inputs are finite; a program needn't handle non-finite values.
Results may differ from a plain program's by a relative error of at most 0.00097.
Values sent between devices are 32-bit elements; how exact they have to be, the bound alone decides.
A program may use at most 64 MiB of HBM per device.

v0:
```python
import jax
import jax.numpy as jnp
from jax import lax
from jax.sharding import PartitionSpec as P

S = 54


def shifted(value, axis, steps):
    count = lax.axis_size(axis)
    pairs = [(source, (source + steps) % count) for source in range(count)]
    return lax.ppermute(value, axis, pairs)


def shards(
    species, weight, destination, slot, counts, cell_index, mix_rate, rate_matrix, rate_bias
):
    particles = species.shape[1]
    block_cap = particles // 6
    owned = mix_rate.shape[0]
    slab_cells = 2 * owned
    slab = lax.axis_index("space")
    nspace = lax.axis_size("space")
    devices = nspace * lax.axis_size("sub")
    for section in range(2):
        target_dev = destination[section]
        place = slot[section]
        block = (target_dev - 2 * slab + 2) % devices
        picked = jnp.sum(
            jnp.where(block[:, None] == jnp.arange(6)[None, :], counts[section][None, :], 0), axis=1
        )
        live = (place < picked).astype(jnp.float32)
        carried = jnp.concatenate([species, (weight * live)[None]], 0)
        column = block * block_cap + place
        outgoing = jnp.zeros((S + 1, 6 * block_cap), jnp.float32).at[:, column].set(carried)
        outgoing = outgoing.reshape(S + 1, 3, 2, block_cap)
        paired = lax.all_to_all(outgoing, "sub", split_axis=2, concat_axis=2, tiled=True)
        lower_part = shifted(paired[:, 2], "space", 1)
        upper_part = shifted(paired[:, 0], "space", -1)
        moved = jnp.concatenate([lower_part, paired[:, 1], upper_part], 1).reshape(
            S + 1, 6 * block_cap
        )
        species = moved[:S]
        weight = moved[S]
        cells = cell_index[section]
        weighted = jnp.concatenate([species * weight[None], weight[None]], 0)
        partial_value = jax.vmap(
            lambda values: jax.ops.segment_sum(values, cells, num_segments=slab_cells)
        )(weighted)
        sums = lax.psum_scatter(partial_value, "sub", scatter_dimension=1, tiled=True)
        mean = sums[:S] / jnp.maximum(sums[S], 1.0)[None]
        table = lax.all_gather(
            jnp.concatenate([mean, mix_rate[None]], 0), "sub", axis=1, tiled=True
        )
        looked_up = jnp.take(table, cells, axis=1)
        local_mean = looked_up[:S]
        mixed = local_mean + (species - local_mean) * jnp.exp(-looked_up[S])[None]
        rate = jnp.dot(rate_matrix, mixed.astype(jnp.bfloat16), preferred_element_type=jnp.float32)
        species = mixed + 0.5 * jnp.tanh(rate + rate_bias[:, None])
    return (species, weight)


def solution(mesh):
    placed = (
        P(None, ("space", "sub")),
        P(("space", "sub")),
        P(None, ("space", "sub")),
        P(None, ("space", "sub")),
        P(None, ("space", "sub")),
        P(None, ("space", "sub")),
        P(("space", "sub")),
        P(),
        P(),
    )
    return jax.shard_map(
        shards,
        mesh=mesh,
        in_specs=placed,
        out_specs=(P(None, ("space", "sub")), P(("space", "sub"))),
        check_vma=False,
    )
```

profile of v0, /device:TPU:1, one launch (start us, length us, event | category | flops | bytes accessed | tf_op | source)
XLA Modules:
  0.0 182.0 jit_solution(14815488996126692281)
XLA Ops:
  7.2 0.7 slice.95
  8.0 1.0 compare_select_fusion
  9.0 0.8 slice_bitcast_fusion.6
  9.7 0.1 select_reduce_fusion.1
  9.8 0.7 compare_select_fusion.9
  10.5 1.2 maximum_bitcast_fusion
  11.7 0.5 copy.47
  12.2 8.5 %scatter_custom_fusion = f32[55,3072]{0,1:T(8,128)S(1)} fusion(s32[3072]{0:T(1024)S(1)} %bitcast.118, f32[3072,55]{1,0:T(8,128)S(1)} %copy.47, f32[]{:T(128)} %constant.24.clone.1), kind=kCustom, calls=%fused_computation.18 | custom fusion | bytes 675844 | tf_op jit(solution)/shard_map/scatter | solution.py:35
  20.7 0.5 copy.48
  21.2 10.9 %all_to_all.10 = f32[55,3,2,512]{3,0,1,2:T(8,128)S(1)} all-to-all(f32[55,3,2,512]{3,0,1,2:T(8,128)S(1)} %copy.48), channel_id=1, replica_groups=mesh['space'=256,'sub'=2] {'sub'}, dimensions={2} | all-to-all | bytes 1351680 | tf_op jit(solution)/shard_map/all_to_all | solution.py:37
  32.2 1.9 %collective-permute-start = (f32[55,2,512]{2,0,1:T(8,128)S(1)}, f32[55,2,512]{2,0,1:T(8,128)S(1)}, u32[]{:S(2)}, u32[]{:S(2)}) collective-permute-start(f32[55,2,512]{2,0,1:T(8,128)S(1)} %get-tuple-element.10), channel_id=1, source_target_pairs={{0,2},{2,4},{4,6},{6,8},{8,10},{10,12},{12,14},{14,16},{16,18},{18... | collective-permute-start | bytes 675848 | tf_op jit(solution)/shard_map/ppermute | solution.py:12
  34.1 10.4 %collective-permute-start.1 = (f32[55,2,512]{2,0,1:T(8,128)S(1)}, f32[55,2,512]{2,0,1:T(8,128)S(1)}, u32[]{:S(2)}, u32[]{:S(2)}) collective-permute-start(f32[55,2,512]{2,0,1:T(8,128)S(1)} %get-tuple-element.11), channel_id=1, source_target_pairs={{0,510},{2,0},{4,2},{6,4},{8,6},{10,8},{12,10},{14,12},{16,14},{18... | collective-permute-start | bytes 675848 | tf_op jit(solution)/shard_map/ppermute | solution.py:12
  44.6 0.1 select_reduce_fusion
  44.7 0.1 copy.53
  44.9 3.3 %collective-permute-done = f32[55,2,512]{2,0,1:T(8,128)S(1)} collective-permute-done((f32[55,2,512]{2,0,1:T(8,128)S(1)}, f32[55,2,512]{2,0,1:T(8,128)S(1)}, u32[]{:S(2)}, u32[]{:S(2)}) %collective-permute-start) | collective-permute-done | bytes 225312 | tf_op jit(solution)/shard_map/ppermute | solution.py:12
  48.2 0.9 collective-permute-done.1
  49.1 0.4 copy.51
  49.6 0.4 copy.67
  50.2 0.5 copy.52
  50.7 17.6 %scatter_custom_fusion.1 = f32[55,512]{0,1:T(8,128)} fusion(s32[3072]{0:T(1024)S(1)} %bitcast.109, f32[3072,55]{1,0:T(8,128)S(1)} %copy.52, f32[]{:T(128)} %constant.24.clone.1), kind=kCustom, calls=%fused_computation.52 | custom fusion | flops 168960 | bytes 112644 | tf_op jit(solution)/shard_map/vmap()/scatter-add | solution.py:48
  68.4 14.2 %reduce-scatter.3.cloned.1.call-done = f32[55,256]{0,1:T(8,128)} async-done(((f32[55,512]{0,1:T(8,128)}), f32[55,256]{0,1:T(8,128)}) %reduce-scatter.3.cloned.1.call-update) | async-done | bytes 56336 | tf_op jit(solution)/shard_map/reduce_scatter | solution.py:50
  82.6 1.1 fusion.17
  83.7 1.0 slice_divide_fusion.1
  84.7 0.1 pad_maximum_fusion.2
  84.8 2.0 %all_gather.6 = f32[55,512]{0,1:T(8,128)S(1)} all-gather(f32[55,256]{0,1:T(8,128)S(1)} %pad_maximum_fusion.2), channel_id=1, replica_groups=mesh['space'=256,'sub'=2] {'sub'}, dimensions={1}, use_global_device_ids=true | all-gather | bytes 168960 | tf_op jit(solution)/shard_map/all_gather | solution.py:52
  86.8 8.1 %gather_fusion = f32[3072,55]{1,0:T(8,128)S(1)} fusion(f32[55,512]{0,1:T(8,128)S(1)} %all_gather.6, s32[3072]{0:T(1024)S(1)} %fusion.32), kind=kCustom, calls=%fused_computation.clone | custom fusion | bytes 1363968 | tf_op jit(solution)/shard_map/jit(_take)/gather | solution.py:55
  94.9 0.5 copy.54
  95.6 0.3 fusion.4
  95.9 0.5 copy.55
  96.4 8.5 %scatter_custom_fusion.2 = f32[55,3072]{0,1:T(8,128)S(1)} fusion(s32[3072]{0:T(1024)S(1)} %bitcast.117, f32[3072,55]{1,0:T(8,128)S(1)} %copy.55, f32[]{:T(128)} %constant.24.clone.1), kind=kCustom, calls=%fused_computation.16 | custom fusion | bytes 675844 | tf_op jit(solution)/shard_map/scatter | solution.py:35
  105.0 0.5 copy.56
  105.5 4.0 %all_to_all.11 = f32[55,3,2,512]{3,0,1,2:T(8,128)S(1)} all-to-all(f32[55,3,2,512]{3,0,1,2:T(8,128)S(1)} %copy.56), channel_id=1, replica_groups=mesh['space'=256,'sub'=2] {'sub'}, dimensions={2} | all-to-all | bytes 1351680 | tf_op jit(solution)/shard_map/all_to_all | solution.py:37
  109.5 2.1 %collective-permute-start.2 = (f32[55,2,512]{2,0,1:T(8,128)S(1)}, f32[55,2,512]{2,0,1:T(8,128)S(1)}, u32[]{:S(2)}, u32[]{:S(2)}) collective-permute-start(f32[55,2,512]{2,0,1:T(8,128)S(1)} %get-tuple-element.7), channel_id=1, source_target_pairs={{0,2},{2,4},{4,6},{6,8},{8,10},{10,12},{12,14},{14,16},{16,18},{18... | collective-permute-start | bytes 675848 | tf_op jit(solution)/shard_map/ppermute | solution.py:12
  111.7 9.0 %collective-permute-start.3 = (f32[55,2,512]{2,0,1:T(8,128)S(1)}, f32[55,2,512]{2,0,1:T(8,128)S(1)}, u32[]{:S(2)}, u32[]{:S(2)}) collective-permute-start(f32[55,2,512]{2,0,1:T(8,128)S(1)} %get-tuple-element.8), channel_id=1, source_target_pairs={{0,510},{2,0},{4,2},{6,4},{8,6},{10,8},{12,10},{14,12},{16,14},{18... | collective-permute-start | bytes 675848 | tf_op jit(solution)/shard_map/ppermute | solution.py:12
  120.7 3.4 %collective-permute-done.2 = f32[55,2,512]{2,0,1:T(8,128)S(1)} collective-permute-done((f32[55,2,512]{2,0,1:T(8,128)S(1)}, f32[55,2,512]{2,0,1:T(8,128)S(1)}, u32[]{:S(2)}, u32[]{:S(2)}) %collective-permute-start.2) | collective-permute-done | bytes 225312 | tf_op jit(solution)/shard_map/ppermute | solution.py:12
  124.1 0.9 collective-permute-done.3
  125.0 0.4 copy.59
  125.5 0.4 copy.68
  126.1 0.5 copy.60
  126.6 17.6 %scatter_custom_fusion.3 = f32[55,512]{0,1:T(8,128)} fusion(s32[3072]{0:T(1024)S(1)} %bitcast.104, f32[3072,55]{1,0:T(8,128)S(1)} %copy.60, f32[]{:T(128)} %constant.24.clone.1), kind=kCustom, calls=%fused_computation.50 | custom fusion | flops 168960 | bytes 112644 | tf_op jit(solution)/shard_map/vmap()/scatter-add | solution.py:48
  144.3 16.8 %reduce-scatter.5.cloned.1.call-done = f32[55,256]{0,1:T(8,128)} async-done(((f32[55,512]{0,1:T(8,128)}), f32[55,256]{0,1:T(8,128)}) %reduce-scatter.5.cloned.1.call-update) | async-done | bytes 56336 | tf_op jit(solution)/shard_map/reduce_scatter | solution.py:50
  161.0 1.1 fusion.16
  162.1 1.0 slice_divide_fusion
  163.2 0.1 pad_maximum_fusion.3
  163.3 2.0 %all_gather.7 = f32[55,512]{0,1:T(8,128)S(1)} all-gather(f32[55,256]{0,1:T(8,128)S(1)} %pad_maximum_fusion.3), channel_id=1, replica_groups=mesh['space'=256,'sub'=2] {'sub'}, dimensions={1}, use_global_device_ids=true | all-gather | bytes 168960 | tf_op jit(solution)/shard_map/all_gather | solution.py:52
  165.3 8.1 %gather_fusion.1 = f32[3072,55]{1,0:T(8,128)S(1)} fusion(f32[55,512]{0,1:T(8,128)S(1)} %all_gather.7, s32[3072]{0:T(1024)S(1)} %fusion.33), kind=kCustom, calls=%fused_computation.1.clone | custom fusion | bytes 1363968 | tf_op jit(solution)/shard_map/jit(_take)/gather | solution.py:55
  173.4 0.5 copy.62
  174.0 1.1 fusion.7
  (41 shorter events, 1.1 us)
Async XLA Ops:
  7.2 88.4 %copy-start = (bf16[54,54]{1,0:T(8,128)(2,1)S(1)}, bf16[54,54]{1,0:T(8,128)(2,1)}, u32[]{:S(2)}) copy-start(bf16[54,54]{1,0:T(8,128)(2,1)} %param.18) | copy-start | bytes 17500
  7.2 75.4 %reduce-scatter.3.cloned.1.call-start = ((), (), s32[]{:S(2)}) async-start(), calls=%async_computation.4 | async-start | bytes 393216 | tf_op jit(solution)/shard_map/reduce_scatter | solution.py:50
  21.2 23.3 %copy-start.3 = (s32[2,3072]{1,0:T(2,128)S(1)}, s32[2,3072]{1,0:T(2,128)}, u32[]{:S(2)}) copy-start(s32[2,3072]{1,0:T(2,128)} %param.16) | copy-start | bytes 73732
  21.2 23.5 %copy-start.5 = (f32[256]{0:T(256)S(1)}, f32[256]{0:T(256)}, u32[]{:S(2)}) copy-start(f32[256]{0:T(256)} %param.17) | copy-start | bytes 3076
  32.2 16.0 %collective-permute-start = (f32[55,2,512]{2,0,1:T(8,128)S(1)}, f32[55,2,512]{2,0,1:T(8,128)S(1)}, u32[]{:S(2)}, u32[]{:S(2)}) collective-permute-start(f32[55,2,512]{2,0,1:T(8,128)S(1)} %get-tuple-element.10), channel_id=1, source_target_pairs={{0,2},{2,4},{4,6},{6,8},{8,10},{10,12},{12,14},{14,16},{16,18},{18... | collective-permute-start | bytes 675848 | tf_op jit(solution)/shard_map/ppermute | solution.py:12
  34.1 15.0 %collective-permute-start.1 = (f32[55,2,512]{2,0,1:T(8,128)S(1)}, f32[55,2,512]{2,0,1:T(8,128)S(1)}, u32[]{:S(2)}, u32[]{:S(2)}) collective-permute-start(f32[55,2,512]{2,0,1:T(8,128)S(1)} %get-tuple-element.11), channel_id=1, source_target_pairs={{0,510},{2,0},{4,2},{6,4},{8,6},{10,8},{12,10},{14,12},{16,14},{18... | collective-permute-start | bytes 675848 | tf_op jit(solution)/shard_map/ppermute | solution.py:12
  50.2 18.2 %copy-start.2 = (s32[2,3072]{1,0:T(2,128)S(1)}, s32[2,3072]{1,0:T(2,128)}, u32[]{:S(2)}) copy-start(s32[2,3072]{1,0:T(2,128)} %param.14) | copy-start | bytes 73732
  68.3 92.7 %reduce-scatter.5.cloned.1.call-start = ((), (), s32[]{:S(2)}) async-start(), calls=%async_computation.5 | async-start | bytes 393216 | tf_op jit(solution)/shard_map/reduce_scatter | solution.py:50
  94.9 0.7 copy-start.4
  109.5 14.5 %collective-permute-start.2 = (f32[55,2,512]{2,0,1:T(8,128)S(1)}, f32[55,2,512]{2,0,1:T(8,128)S(1)}, u32[]{:S(2)}, u32[]{:S(2)}) collective-permute-start(f32[55,2,512]{2,0,1:T(8,128)S(1)} %get-tuple-element.7), channel_id=1, source_target_pairs={{0,2},{2,4},{4,6},{6,8},{8,10},{10,12},{12,14},{14,16},{16,18},{18... | collective-permute-start | bytes 675848 | tf_op jit(solution)/shard_map/ppermute | solution.py:12
  111.7 13.3 %collective-permute-start.3 = (f32[55,2,512]{2,0,1:T(8,128)S(1)}, f32[55,2,512]{2,0,1:T(8,128)S(1)}, u32[]{:S(2)}, u32[]{:S(2)}) collective-permute-start(f32[55,2,512]{2,0,1:T(8,128)S(1)} %get-tuple-element.8), channel_id=1, source_target_pairs={{0,510},{2,0},{4,2},{6,4},{8,6},{10,8},{12,10},{14,12},{16,14},{18... | collective-permute-start | bytes 675848 | tf_op jit(solution)/shard_map/ppermute | solution.py:12
  126.0 0.7 copy-start.1
Sparse Core Ops, SparseCore 0:
  68.4 14.1 reduce-scatter.2
  144.3 16.6 reduce-scatter.4
where the time goes:
time: 183 us; the launch traced here: 182 us
  other arithmetic  43.2 us (24%)
  local copies, waits for them, and re-layouts  40.9 us (22%)
  waiting for transfers between devices  39.6 us (22%)
  starting transfers between devices  23.5 us (13%)
  blocking collectives  18.9 us (10%)
  between operations  14.5 us (8%)
    scatter-add x2, other arithmetic, shards(): jax.ops.segment_sum(values, cells, num_segments=slab_cells)  35.2 us
    reduce_scatter x2, waiting for transfers between devices, shards(): lax.psum_scatter(partial_value, 'sub', scatter_dimension=1, tiled=True)  31 us
    ppermute x4, starting transfers between devices, shifted(): return lax.ppermute(value, axis, pairs)  23.4 us
    gather x4, local copies, waits for them, and re-layouts, shards(): looked_up = jnp.take(table, cells, axis=1)  17.2 us
    scatter x2, local copies, waits for them, and re-layouts, shards(): jnp.zeros((S + 1, 6 * block_cap), jnp.float32).at[:, column].set(carried)  17 us
    all_to_all x2, blocking collectives, shards(): lax.all_to_all(outgoing, 'sub', split_axis=2, concat_axis=2, tiled=True)  14.9 us
    ppermute x4, waiting for transfers between devices, shifted(): return lax.ppermute(value, axis, pairs)  8.54 us
    all_gather x2, blocking collectives, shards(): lax.all_gather(jnp.concatenate([mean, mix_rate[None]], 0), 'sub', axis=1,...  3.99 us
  transfers between devices with their start and end apart: 6, of which 6 were waited for; matrix products, arithmetic and copies ran while one was open for 0% of the time, Pallas kernels for 0%

commit v1 on v0

v1 whole, which is shorter than its diff:
```python
import functools

import jax
import jax.numpy as jnp
from jax import lax
from jax.experimental import pallas as pl
from jax.experimental.pallas import tpu as pltpu
from jax.sharding import PartitionSpec as P

S = 54
R = 56
CAP = 512
N = 6 * CAP
CELLS = 512
KC = 256
MESH = pl.DeviceIdType.MESH


def split(value):
    high = value.astype(jnp.bfloat16).astype(jnp.float32)
    return jnp.concatenate([high, value - high], 0).astype(jnp.bfloat16)


def joined(value):
    return value[:R] + value[R:]


def spread(row, out):
    for c in range(N // 128):
        chunk = jnp.broadcast_to(row[:, c * 128 : (c + 1) * 128], (128, 128))
        out[c * 128 : (c + 1) * 128, :] = chunk.T


def hot_lanes(spread_rows, base, width):
    parts = []
    for part in range(width // 128):
        lanes = lax.broadcasted_iota(jnp.int32, (1, 128), 1) + (base + part * 128)
        parts.append(
            jnp.where(
                spread_rows == jnp.broadcast_to(lanes, spread_rows.shape), 1.0, 0.0
            ).astype(jnp.bfloat16)
        )
    return jnp.concatenate(parts, 1)


def hot_rows(row, base, depth):
    rows = lax.broadcasted_iota(jnp.int32, (depth, row.shape[1]), 0) + base
    return jnp.where(rows == jnp.broadcast_to(row, rows.shape), 1.0, 0.0).astype(jnp.bfloat16)


def kernel(
    nspace,
    species,
    weight,
    destination,
    slot,
    counts,
    cell_index,
    mix_rate,
    matrix,
    bias,
    species_out,
    weight_out,
    taken,
    parts,
    col_b,
    cell_b,
    sending,
    landed,
    sums,
    sums_in,
    rates,
    load_sem,
    send_sem,
    recv_sem,
    sum_send,
    sum_recv,
    rate_send,
    rate_recv,
):
    slab = lax.axis_index("space")
    sub = lax.axis_index("sub")
    other = 1 - sub
    before = lax.rem(slab + nspace - 1, nspace)
    after = lax.rem(slab + 1, nspace)
    devices = 2 * nspace

    load = pltpu.make_async_copy(species, taken, load_sem)
    load.start()
    barrier = pltpu.get_barrier_semaphore()
    peers = ((before, sub), (before, other), (after, sub), (after, other), (slab, other))
    for peer in peers:
        pl.semaphore_signal(barrier, inc=1, device_id=peer, device_id_type=MESH)

    def routing(step):
        target = destination[step : step + 1, :]
        place = slot[step : step + 1, :]
        block = jnp.bitwise_and(target - 2 * slab + 2 + devices, devices - 1)
        picked = jnp.zeros_like(place)
        for b in range(6):
            picked = jnp.where(block == b, counts[step, b], picked)
        live = jnp.where(place < picked, 1.0, 0.0)
        return block * CAP + place, live

    def permuted(block):
        total = jnp.zeros((2 * R, CAP), jnp.float32)
        for k in range(N // KC):
            hot = hot_lanes(col_b[k * KC : (k + 1) * KC, :], block * CAP, CAP)
            total = total + jnp.dot(
                parts[:, k * KC : (k + 1) * KC], hot, preferred_element_type=jnp.float32
            )
        return joined(total)

    def sent(step, i):
        kind = (2, 0, 2, 0, 1)[i]
        peer_sub = (sub, sub, other, other, other)[i]
        peer_slab = (before, slab, after)[kind]
        land = 2 * (2 - kind) + sub
        copy = pltpu.make_async_remote_copy(
            src_ref=sending.at[step, i],
            dst_ref=landed.at[step, land],
            send_sem=send_sem.at[step, i],
            recv_sem=recv_sem.at[step, land],
            device_id=(peer_slab, peer_sub),
            device_id_type=MESH,
        )
        return 2 * kind + peer_sub, copy

    def arrived(step, land):
        pltpu.make_async_remote_copy(
            src_ref=sending.at[step, 0],
            dst_ref=landed.at[step, land],
            send_sem=send_sem.at[step, 0],
            recv_sem=recv_sem.at[step, land],
            device_id=(slab, other),
            device_id_type=MESH,
        ).wait_recv()

    rate_copy = pltpu.make_async_remote_copy(
        src_ref=mix_rate,
        dst_ref=rates.at[sub],
        send_sem=rate_send,
        recv_sem=rate_recv,
        device_id=(slab, other),
        device_id_type=MESH,
    )

    def exchange(step):
        return pltpu.make_async_remote_copy(
            src_ref=sums.at[step],
            dst_ref=sums_in.at[step],
            send_sem=sum_send.at[step],
            recv_sem=sum_recv.at[step],
            device_id=(slab, other),
            device_id_type=MESH,
        )

    column, live = routing(0)
    spread(column, col_b)
    load.wait()
    for j in range(6):
        here = slice(j * CAP, (j + 1) * CAP)
        parts[:, here] = split(
            jnp.concatenate(
                [
                    taken[:, here],
                    weight[:, here] * live[:, here],
                    jnp.zeros((1, CAP), jnp.float32),
                ],
                0,
            )
        )
    rates[sub] = mix_rate[...]
    eye = lax.broadcasted_iota(jnp.int32, (S, S), 0) == lax.broadcasted_iota(jnp.int32, (S, S), 1)
    bias_column = jnp.sum(jnp.where(eye, bias[...], 0.0), axis=1, keepdims=True)
    last_row = lax.broadcasted_iota(jnp.int32, (R, 1), 0) == S

    for step in range(2):
        for i in range(5):
            block, copy = sent(step, i)
            sending[step, i] = permuted(block)
            if step == 0 and i == 0:
                pl.semaphore_wait(barrier, 5)
            copy.start()
            if step == 0 and i == 0:
                rate_copy.start()
        landed[step, 2 + sub] = permuted(2 + sub)

        cells = cell_index[step : step + 1, :]
        spread(cells, cell_b)
        if step == 0:
            rate_copy.wait()
            column, live = routing(1)
            spread(column, col_b)
        decay = jnp.exp(-jnp.concatenate([rates[0], rates[1]], 1))

        total = jnp.zeros((2 * R, CELLS), jnp.float32)
        order = (2 + sub, 2 + other, sub, 4 + sub, other, 4 + other)
        for place, land in enumerate(order):
            if place > 0:
                arrived(step, land)
            value = landed[step, land]
            mass = value[S : S + 1]
            weighted = split(jnp.where(last_row, mass, value * mass))
            for k in range(CAP // KC):
                rows = pl.ds(pl.multiple_of(land * CAP + k * KC, KC), KC)
                total = total + jnp.dot(
                    weighted[:, k * KC : (k + 1) * KC],
                    hot_lanes(cell_b[rows, :], 0, CELLS),
                    preferred_element_type=jnp.float32,
                )
        mine = joined(total)
        sums[step] = mine
        swap = exchange(step)
        swap.start()
        swap.wait()
        whole = mine + sums_in[step]
        mean = whole / jnp.maximum(whole[S : S + 1], 1.0)
        table = split(jnp.where(last_row, decay, mean * (1.0 - decay)))
        for j in range(6):
            here = slice(j * CAP, (j + 1) * CAP)
            looked = jnp.zeros((2 * R, CAP), jnp.float32)
            for k in range(CELLS // KC):
                looked = looked + jnp.dot(
                    table[:, k * KC : (k + 1) * KC],
                    hot_rows(cells[:, here], k * KC, KC),
                    preferred_element_type=jnp.float32,
                )
            looked = joined(looked)
            value = landed[step, j]
            mixed = (looked + value * looked[S : S + 1])[:S]
            rate = jnp.dot(
                matrix[...], mixed.astype(jnp.bfloat16), preferred_element_type=jnp.float32
            )
            fresh = mixed + 0.5 * jnp.tanh(rate + bias_column)
            mass = value[S : S + 1]
            if step == 0:
                parts[:, here] = split(
                    jnp.concatenate(
                        [fresh, mass * live[:, here], jnp.zeros((1, CAP), jnp.float32)], 0
                    )
                )
            else:
                species_out[:, here] = fresh
                weight_out[:, here] = mass
        for i in range(5):
            sent(step, i)[1].wait_send()


def shards(
    species, weight, destination, slot, counts, cell_index, mix_rate, rate_matrix, rate_bias
):
    nspace = lax.axis_size("space")
    vmem = pl.BlockSpec(memory_space=pltpu.VMEM)
    out = pl.pallas_call(
        functools.partial(kernel, nspace),
        out_shape=(
            jax.ShapeDtypeStruct((S, N), jnp.float32),
            jax.ShapeDtypeStruct((1, N), jnp.float32),
        ),
        in_specs=[
            pl.BlockSpec(memory_space=pl.ANY),
            vmem,
            vmem,
            vmem,
            pl.BlockSpec(memory_space=pltpu.SMEM),
            vmem,
            vmem,
            vmem,
            vmem,
        ],
        out_specs=(vmem, vmem),
        scratch_shapes=[
            pltpu.VMEM((S, N), jnp.float32),
            pltpu.VMEM((2 * R, N), jnp.bfloat16),
            pltpu.VMEM((N, 128), jnp.int32),
            pltpu.VMEM((N, 128), jnp.int32),
            pltpu.VMEM((2, 5, R, CAP), jnp.float32),
            pltpu.VMEM((2, 6, R, CAP), jnp.float32),
            pltpu.VMEM((2, R, CELLS), jnp.float32),
            pltpu.VMEM((2, R, CELLS), jnp.float32),
            pltpu.VMEM((2, 1, 256), jnp.float32),
            pltpu.SemaphoreType.DMA,
            pltpu.SemaphoreType.DMA((2, 5)),
            pltpu.SemaphoreType.DMA((2, 6)),
            pltpu.SemaphoreType.DMA((2,)),
            pltpu.SemaphoreType.DMA((2,)),
            pltpu.SemaphoreType.DMA,
            pltpu.SemaphoreType.DMA,
        ],
        compiler_params=pltpu.CompilerParams(
            collective_id=0, has_side_effects=True, vmem_limit_bytes=48 * 1024 * 1024
        ),
    )(
        species,
        weight[None],
        destination,
        slot,
        counts,
        cell_index,
        mix_rate[None],
        rate_matrix,
        rate_bias[None],
    )
    return out[0], out[1][0]


def solution(mesh):
    placed = (
        P(None, ("space", "sub")),
        P(("space", "sub")),
        P(None, ("space", "sub")),
        P(None, ("space", "sub")),
        P(None, ("space", "sub")),
        P(None, ("space", "sub")),
        P(("space", "sub")),
        P(),
        P(),
    )
    return jax.shard_map(
        shards,
        mesh=mesh,
        in_specs=placed,
        out_specs=(P(None, ("space", "sub")), P(("space", "sub"))),
        check_vma=False,
    )
```

time: 183 us -> 51.4 us (0.28)
  Pallas kernels: 0 us -> 43.4 us
  other arithmetic: 43.2 us -> 0 us
  waiting for transfers between devices: 39.6 us -> 0 us
  local copies, waits for them, and re-layouts: 40.9 us -> 6.85 us
  starting transfers between devices: 23.5 us -> 0 us
  blocking collectives: 18.9 us -> 0 us
  between operations: 14.5 us -> 0.67 us
    pallas_call x0 -> x1, Pallas kernels: none -> 43.4 us  [shards(): pl.pallas_call(functools.partial(kernel, nspace), out_shape=(jax.ShapeDty...]
    scatter-add x2 -> x0, other arithmetic: 35.2 us -> none  [shards(): jax.ops.segment_sum(values, cells, num_segments=slab_cells)]
    reduce_scatter x2 -> x0, waiting for transfers between devices: 31 us -> none  [shards(): lax.psum_scatter(partial_value, 'sub', scatter_dimension=1, tiled=True)]
    ppermute x4 -> x0, starting transfers between devices: 23.4 us -> none  [shifted(): return lax.ppermute(value, axis, pairs)]
    gather x4 -> x0, local copies, waits for them, and re-layouts: 17.2 us -> none  [shards(): looked_up = jnp.take(table, cells, axis=1)]
    scatter x2 -> x0, local copies, waits for them, and re-layouts: 17 us -> none  [shards(): jnp.zeros((S + 1, 6 * block_cap), jnp.float32).at[:, column].set(carried)]
    all_to_all x2 -> x0, blocking collectives: 14.9 us -> none  [shards(): lax.all_to_all(outgoing, 'sub', split_axis=2, concat_axis=2, tiled=True)]
    ppermute x4 -> x0, waiting for transfers between devices: 8.54 us -> none  [shifted(): return lax.ppermute(value, axis, pairs)]
  transfers between devices with their start and end apart: 6 -> 0, of which waited for: 6 -> 0; matrix products, arithmetic and copies ran while one was open for 0% -> 0% of each run, Pallas kernels for 0% -> 0%
where the time goes in v1:
time: 51.4 us; the launch traced here: 50.9 us
  Pallas kernels  43.4 us (84%)
  local copies, waits for them, and re-layouts  6.85 us (13%)
  between operations  0.67 us (1%)
    pallas_call x1, Pallas kernels, shards(): pl.pallas_call(functools.partial(kernel, nspace), out_shape=(jax.ShapeDty...  43.4 us
    unnamed x20, local copies, waits for them, and re-layouts  6.85 us

profile of v1, /device:TPU:1, one launch (start us, length us, event | category | flops | bytes accessed | tf_op | source)
XLA Modules:
  0.0 50.9 jit_solution(11191727920596589308)
XLA Ops:
  0.6 0.0 copy-start.7
  0.6 0.0 copy-start.6
  0.7 0.0 copy-start.8
  0.7 0.7 %copy-done.7 = f32[256]{0:T(256)S(1)} copy-done((f32[256]{0:T(256)S(1)}, f32[256]{0:T(256)}, u32[]{:S(2)}) %copy-start.7) | copy-done | bytes 1048
  1.3 0.0 copy-done.6
  1.3 0.0 copy-done.8
  1.3 0.0 copy-start
  1.3 1.1 %copy-done = f32[54,3072]{1,0:T(8,128)S(1)} copy-done((f32[54,3072]{1,0:T(8,128)S(1)}, f32[54,3072]{1,0:T(8,128)}, u32[]{:S(2)}) %copy-start) | copy-done | bytes 663576
  2.4 0.0 copy-start.1
  2.4 0.7 %copy-done.1 = s32[2,3072]{1,0:T(2,128)S(1)} copy-done((s32[2,3072]{1,0:T(2,128)S(1)}, s32[2,3072]{1,0:T(2,128)}, u32[]{:S(2)}) %copy-start.1) | copy-done | bytes 24600
  3.2 0.0 copy-start.2
  3.2 0.7 %copy-done.2 = s32[2,3072]{1,0:T(2,128)S(1)} copy-done((s32[2,3072]{1,0:T(2,128)S(1)}, s32[2,3072]{1,0:T(2,128)}, u32[]{:S(2)}) %copy-start.2) | copy-done | bytes 24600
  3.9 0.0 copy-start.3
  3.9 0.7 %copy-done.3 = s32[2,3072]{1,0:T(2,128)S(1)} copy-done((s32[2,3072]{1,0:T(2,128)S(1)}, s32[2,3072]{1,0:T(2,128)}, u32[]{:S(2)}) %copy-start.3) | copy-done | bytes 24600
  4.6 0.0 copy-start.4
  4.6 0.7 %copy-done.4 = bf16[54,54]{1,0:T(8,128)(2,1)S(1)} copy-done((bf16[54,54]{1,0:T(8,128)(2,1)S(1)}, bf16[54,54]{1,0:T(8,128)(2,1)}, u32[]{:S(2)}) %copy-start.4) | copy-done | bytes 5856
  5.4 0.0 copy-start.5
  5.4 0.7 %copy-done.5 = f32[3072]{0:T(1024)S(1)} copy-done((f32[3072]{0:T(1024)S(1)}, f32[3072]{0:T(1024)}, u32[]{:S(2)}) %copy-start.5) | copy-done | bytes 12312
  6.1 43.4 %shard_map.104 = (f32[54,3072]{1,0:T(8,128)S(1)}, f32[1,3072]{1,0:T(1,128)S(1)}) custom-call(f32[54,3072]{1,0:T(8,128)S(1)} %copy-done, f32[1,3072]{1,0:T(1,128)S(1)} %bitcast.5, s32[2,3072]{1,0:T(2,128)S(1)} %copy-done.1, s32[2,3072]{1,0:T(2,128)S(1)} %copy-done.2, s32[2,6]{1,0:T(2,128)S(1)} %copy-done.6, s32[2,3072]{1,0:T(2,128)S(1)} %copy-done.3, ...), custom_call_target="tpu_custom_call" | custom-call | tf_op jit(solution)/shard_map/pallas_call | solution.py:255
  49.5 0.8 %copy.13 = f32[54,3072]{1,0:T(8,128)} copy(f32[54,3072]{1,0:T(8,128)S(1)} %get-tuple-element.8) | data formatting | bytes 1327104
  50.3 0.6 %copy.14 = f32[3072]{0:T(1024)} copy(f32[3072]{0:T(1024)S(1)} %bitcast.4) | data formatting | bytes 24576
Async XLA Ops:
  0.6 0.7 %copy-start.7 = (f32[256]{0:T(256)S(1)}, f32[256]{0:T(256)}, u32[]{:S(2)}) copy-start(f32[256]{0:T(256)} %param.15) | copy-start | bytes 3076
  0.6 0.7 %copy-start.6 = (s32[2,6]{1,0:T(2,128)S(1)}, s32[2,6]{1,0:T(2,128)}, u32[]{:S(2)}) copy-start(s32[2,6]{1,0:T(2,128)} %counts.1) | copy-start | bytes 148
  0.7 0.7 %copy-start.8 = (f32[54]{0:T(128)S(1)}, f32[54]{0:T(128)}, u32[]{:S(2)}) copy-start(f32[54]{0:T(128)} %param.17) | copy-start | bytes 652
  1.3 1.1 %copy-start = (f32[54,3072]{1,0:T(8,128)S(1)}, f32[54,3072]{1,0:T(8,128)}, u32[]{:S(2)}) copy-start(f32[54,3072]{1,0:T(8,128)} %species.1) | copy-start | bytes 1990660
  2.4 0.7 %copy-start.1 = (s32[2,3072]{1,0:T(2,128)S(1)}, s32[2,3072]{1,0:T(2,128)}, u32[]{:S(2)}) copy-start(s32[2,3072]{1,0:T(2,128)} %destination.1) | copy-start | bytes 73732
  3.2 0.7 %copy-start.2 = (s32[2,3072]{1,0:T(2,128)S(1)}, s32[2,3072]{1,0:T(2,128)}, u32[]{:S(2)}) copy-start(s32[2,3072]{1,0:T(2,128)} %slot.1) | copy-start | bytes 73732
  3.9 0.7 %copy-start.3 = (s32[2,3072]{1,0:T(2,128)S(1)}, s32[2,3072]{1,0:T(2,128)}, u32[]{:S(2)}) copy-start(s32[2,3072]{1,0:T(2,128)} %cell_index.1) | copy-start | bytes 73732
  4.6 0.7 %copy-start.4 = (bf16[54,54]{1,0:T(8,128)(2,1)S(1)}, bf16[54,54]{1,0:T(8,128)(2,1)}, u32[]{:S(2)}) copy-start(bf16[54,54]{1,0:T(8,128)(2,1)} %matrix.1) | copy-start | bytes 17500
  5.4 0.7 %copy-start.5 = (f32[3072]{0:T(1024)S(1)}, f32[3072]{0:T(1024)}, u32[]{:S(2)}) copy-start(f32[3072]{0:T(1024)} %param.10) | copy-start | bytes 36868

commit v2 on v1

--- a/solution.py
+++ b/solution.py
@@ -51,6 +51,17 @@
 def kernel(
     nspace,
     species,
+    weight_in,
+    destination_in,
+    slot_in,
+    counts_in,
+    cell_in,
+    rate_in,
+    matrix_in,
+    bias_in,
+    species_out,
+    weight_out,
+    taken,
     weight,
     destination,
     slot,
@@ -59,9 +70,6 @@
     mix_rate,
     matrix,
     bias,
-    species_out,
-    weight_out,
-    taken,
     parts,
     col_b,
     cell_b,
@@ -85,12 +93,25 @@
     after = lax.rem(slab + 1, nspace)
     devices = 2 * nspace
 
-    load = pltpu.make_async_copy(species, taken, load_sem)
-    load.start()
     barrier = pltpu.get_barrier_semaphore()
     peers = ((before, sub), (before, other), (after, sub), (after, other), (slab, other))
     for peer in peers:
         pl.semaphore_signal(barrier, inc=1, device_id=peer, device_id_type=MESH)
+    loads = []
+    for source, target in (
+        (destination_in, destination),
+        (slot_in, slot),
+        (counts_in, counts),
+        (species, taken),
+        (weight_in, weight),
+        (cell_in, cell_index),
+        (rate_in, mix_rate),
+        (matrix_in, matrix),
+        (bias_in, bias),
+    ):
+        load = pltpu.make_async_copy(source, target, load_sem.at[len(loads)])
+        load.start()
+        loads.append(load)
 
     def routing(step):
         target = destination[step : step + 1, :]
@@ -98,7 +119,8 @@
         block = jnp.bitwise_and(target - 2 * slab + 2 + devices, devices - 1)
         picked = jnp.zeros_like(place)
         for b in range(6):
-            picked = jnp.where(block == b, counts[step, b], picked)
+            count = jnp.broadcast_to(counts[step : step + 1, b : b + 1], place.shape)
+            picked = jnp.where(block == b, count, picked)
         live = jnp.where(place < picked, 1.0, 0.0)
         return block * CAP + place, live
 
@@ -155,9 +177,12 @@
             device_id_type=MESH,
         )
 
+    for load in loads[:3]:
+        load.wait()
     column, live = routing(0)
     spread(column, col_b)
-    load.wait()
+    for load in loads[3:]:
+        load.wait()
     for j in range(6):
         here = slice(j * CAP, (j + 1) * CAP)
         parts[:, here] = split(
@@ -258,20 +283,18 @@
             jax.ShapeDtypeStruct((S, N), jnp.float32),
             jax.ShapeDtypeStruct((1, N), jnp.float32),
         ),
-        in_specs=[
-            pl.BlockSpec(memory_space=pl.ANY),
-            vmem,
-            vmem,
-            vmem,
-            pl.BlockSpec(memory_space=pltpu.SMEM),
-            vmem,
-            vmem,
-            vmem,
-            vmem,
-        ],
+        in_specs=[pl.BlockSpec(memory_space=pltpu.HBM)] * 9,
         out_specs=(vmem, vmem),
         scratch_shapes=[
             pltpu.VMEM((S, N), jnp.float32),
+            pltpu.VMEM((1, N), jnp.float32),
+            pltpu.VMEM((2, N), jnp.int32),
+            pltpu.VMEM((2, N), jnp.int32),
+            pltpu.VMEM((2, 6), jnp.int32),
+            pltpu.VMEM((2, N), jnp.int32),
+            pltpu.VMEM((1, 256), jnp.float32),
+            pltpu.VMEM((S, S), jnp.bfloat16),
+            pltpu.VMEM((1, S), jnp.float32),
             pltpu.VMEM((2 * R, N), jnp.bfloat16),
             pltpu.VMEM((N, 128), jnp.int32),
             pltpu.VMEM((N, 128), jnp.int32),
@@ -280,7 +303,7 @@
             pltpu.VMEM((2, R, CELLS), jnp.float32),
             pltpu.VMEM((2, R, CELLS), jnp.float32),
             pltpu.VMEM((2, 1, 256), jnp.float32),
-            pltpu.SemaphoreType.DMA,
+            pltpu.SemaphoreType.DMA((9,)),
             pltpu.SemaphoreType.DMA((2, 5)),
             pltpu.SemaphoreType.DMA((2, 6)),
             pltpu.SemaphoreType.DMA((2,)),
@@ -289,7 +312,7 @@
             pltpu.SemaphoreType.DMA,
         ],
         compiler_params=pltpu.CompilerParams(
-            collective_id=0, has_side_effects=True, vmem_limit_bytes=48 * 1024 * 1024
+            collective_id=0, has_side_effects=True, vmem_limit_bytes=67043328
         ),
     )(
         species,

time: 51.4 us -> 47 us (0.914)
  local copies, waits for them, and re-layouts: 6.85 us -> 2.6 us
    unnamed x20 -> x4, local copies, waits for them, and re-layouts: 6.85 us -> 2.6 us
where the time goes in v2:
time: 47 us; the launch traced here: 46.9 us
  Pallas kernels  43.6 us (93%)
  local copies, waits for them, and re-layouts  2.6 us (6%)
  between operations  0.65 us (1%)
    pallas_call x1, Pallas kernels, shards(): pl.pallas_call(functools.partial(kernel, nspace), out_shape=(jax.ShapeDty...  43.6 us
    unnamed x4, local copies, waits for them, and re-layouts  2.6 us

profile of v2, /device:TPU:1, one launch (start us, length us, event | category | flops | bytes accessed | tf_op | source)
XLA Modules:
  0.0 46.9 jit_solution(18420710449794508711)
XLA Ops:
  0.6 43.6 %shard_map.104 = (f32[54,3072]{1,0:T(8,128)}, f32[1,3072]{1,0:T(1,128)}) custom-call(f32[54,3072]{1,0:T(8,128)} %species.1, f32[1,3072]{1,0:T(1,128)} %bitcast.5, s32[2,3072]{1,0:T(2,128)} %destination_in.1, s32[2,3072]{1,0:T(2,128)} %slot_in.1, s32[2,6]{1,0:T(2,128)} %counts_in.1, s32[2,3072]{1,0:T(2,128)} %cell_in.1, f32[1,256]{1,0:T(1,128)} %bitcast.6, ...), custom_call_target="tpu_custom_call" | custom-call | tf_op jit(solution)/shard_map/pallas_call | solution.py:280
  44.2 0.0 copy-start
  44.3 2.0 %copy.13 = f32[54,3072]{1,0:T(8,128)} copy(f32[54,3072]{1,0:T(8,128)} %get-tuple-element.8) | data formatting | bytes 1327104
  46.2 0.0 copy-done
  46.2 0.6 %copy.14 = f32[3072]{0:T(1024)} copy(f32[3072]{0:T(1024)S(1)} %bitcast.4) | data formatting | bytes 24576
Async XLA Ops:
  44.2 2.0 %copy-start = (f32[1,3072]{1,0:T(1,128)S(1)}, f32[1,3072]{1,0:T(1,128)}, u32[]{:S(2)}) copy-start(f32[1,3072]{1,0:T(1,128)} %get-tuple-element.5) | copy-start | bytes 36868

commit v3 on v2

--- a/solution.py
+++ b/solution.py
@@ -46,6 +46,45 @@
 def hot_rows(row, base, depth):
     rows = lax.broadcasted_iota(jnp.int32, (depth, row.shape[1]), 0) + base
     return jnp.where(rows == jnp.broadcast_to(row, rows.shape), 1.0, 0.0).astype(jnp.bfloat16)
+
+
+def looked_up(table, cells, j):
+    total = jnp.zeros((2 * R, CAP), jnp.float32)
+    for k in range(CELLS // KC):
+        total = total + jnp.dot(
+            table[:, k * KC : (k + 1) * KC],
+            hot_rows(cells[:, j * CAP : (j + 1) * CAP], k * KC, KC),
+            preferred_element_type=jnp.float32,
+        )
+    return joined(total)
+
+
+def reacted(value, looked, matrix, bias):
+    mixed = (looked + value * looked[S : S + 1])[:S]
+    rate = jnp.dot(matrix, mixed.astype(jnp.bfloat16), preferred_element_type=jnp.float32)
+    return mixed + 0.5 * jnp.tanh(rate + bias)
+
+
+def finish(landed, table_in, cells_in, matrix_in, bias_in, species_out, weight_out, fresh, mass, sem):
+    for j in range(6):
+        mass[:, j * CAP : (j + 1) * CAP] = landed[j, S : S + 1, :]
+    stores = [pltpu.make_async_copy(mass, weight_out, sem.at[6])]
+    stores[0].start()
+    table, cells = table_in[...], cells_in[...]
+    matrix, bias = matrix_in[...], bias_in[...]
+    looked = looked_up(table, cells, 0)
+    for j in range(6):
+        now = looked
+        if j < 5:
+            looked = looked_up(table, cells, j + 1)
+        fresh[:, j * CAP : (j + 1) * CAP] = reacted(landed[j], now, matrix, bias)
+        store = pltpu.make_async_copy(
+            fresh.at[:, pl.ds(j * CAP, CAP)], species_out.at[:, pl.ds(j * CAP, CAP)], sem.at[j]
+        )
+        store.start()
+        stores.append(store)
+    for store in stores:
+        store.wait()
 
 
 def kernel(
@@ -59,8 +98,11 @@
     rate_in,
     matrix_in,
     bias_in,
-    species_out,
-    weight_out,
+    last_landed,
+    last_table,
+    last_cells,
+    matrix_out,
+    bias_out,
     taken,
     weight,
     destination,
@@ -74,7 +116,7 @@
     col_b,
     cell_b,
     sending,
-    landed,
+    first_landed,
     sums,
     sums_in,
     rates,
@@ -92,6 +134,7 @@
     before = lax.rem(slab + nspace - 1, nspace)
     after = lax.rem(slab + 1, nspace)
     devices = 2 * nspace
+    landed = (first_landed, last_landed)
 
     barrier = pltpu.get_barrier_semaphore()
     peers = ((before, sub), (before, other), (after, sub), (after, other), (slab, other))
@@ -140,7 +183,7 @@
         land = 2 * (2 - kind) + sub
         copy = pltpu.make_async_remote_copy(
             src_ref=sending.at[step, i],
-            dst_ref=landed.at[step, land],
+            dst_ref=landed[step].at[land],
             send_sem=send_sem.at[step, i],
             recv_sem=recv_sem.at[step, land],
             device_id=(peer_slab, peer_sub),
@@ -151,7 +194,7 @@
     def arrived(step, land):
         pltpu.make_async_remote_copy(
             src_ref=sending.at[step, 0],
-            dst_ref=landed.at[step, land],
+            dst_ref=landed[step].at[land],
             send_sem=send_sem.at[step, 0],
             recv_sem=recv_sem.at[step, land],
             device_id=(slab, other),
@@ -198,6 +241,9 @@
     rates[sub] = mix_rate[...]
     eye = lax.broadcasted_iota(jnp.int32, (S, S), 0) == lax.broadcasted_iota(jnp.int32, (S, S), 1)
     bias_column = jnp.sum(jnp.where(eye, bias[...], 0.0), axis=1, keepdims=True)
+    last_cells[...] = cell_index[1:2, :]
+    matrix_out[...] = matrix[...]
+    bias_out[...] = bias_column
     last_row = lax.broadcasted_iota(jnp.int32, (R, 1), 0) == S
 
     for step in range(2):
@@ -209,7 +255,7 @@
             copy.start()
             if step == 0 and i == 0:
                 rate_copy.start()
-        landed[step, 2 + sub] = permuted(2 + sub)
+        landed[step][2 + sub] = permuted(2 + sub)
 
         cells = cell_index[step : step + 1, :]
         spread(cells, cell_b)
@@ -224,7 +270,7 @@
         for place, land in enumerate(order):
             if place > 0:
                 arrived(step, land)
-            value = landed[step, land]
+            value = landed[step][land]
             mass = value[S : S + 1]
             weighted = split(jnp.where(last_row, mass, value * mass))
             for k in range(CAP // KC):
@@ -242,32 +288,21 @@
         whole = mine + sums_in[step]
         mean = whole / jnp.maximum(whole[S : S + 1], 1.0)
         table = split(jnp.where(last_row, decay, mean * (1.0 - decay)))
-        for j in range(6):
-            here = slice(j * CAP, (j + 1) * CAP)
-            looked = jnp.zeros((2 * R, CAP), jnp.float32)
-            for k in range(CELLS // KC):
-                looked = looked + jnp.dot(
-                    table[:, k * KC : (k + 1) * KC],
-                    hot_rows(cells[:, here], k * KC, KC),
-                    preferred_element_type=jnp.float32,
+        if step == 0:
+            looked = looked_up(table, cells, 0)
+            for j in range(6):
+                here = slice(j * CAP, (j + 1) * CAP)
+                now = looked
+                if j < 5:
+                    looked = looked_up(table, cells, j + 1)
+                value = first_landed[j]
+                fresh = reacted(value, now, matrix[...], bias_column)
+                mass = value[S : S + 1] * live[:, here]
+                parts[:, here] = split(
+                    jnp.concatenate([fresh, mass, jnp.zeros((1, CAP), jnp.float32)], 0)
                 )
-            looked = joined(looked)
-            value = landed[step, j]
-            mixed = (looked + value * looked[S : S + 1])[:S]
-            rate = jnp.dot(
-                matrix[...], mixed.astype(jnp.bfloat16), preferred_element_type=jnp.float32
-            )
-            fresh = mixed + 0.5 * jnp.tanh(rate + bias_column)
-            mass = value[S : S + 1]
-            if step == 0:
-                parts[:, here] = split(
-                    jnp.concatenate(
-                        [fresh, mass * live[:, here], jnp.zeros((1, CAP), jnp.float32)], 0
-                    )
-                )
-            else:
-                species_out[:, here] = fresh
-                weight_out[:, here] = mass
+        else:
+            last_table[...] = table
         for i in range(5):
             sent(step, i)[1].wait_send()
 
@@ -277,14 +312,29 @@
 ):
     nspace = lax.axis_size("space")
     vmem = pl.BlockSpec(memory_space=pltpu.VMEM)
-    out = pl.pallas_call(
+    hbm = pl.BlockSpec(memory_space=pltpu.HBM)
+    arguments = (
+        species,
+        weight[None],
+        destination,
+        slot,
+        counts,
+        cell_index,
+        mix_rate[None],
+        rate_matrix,
+        rate_bias[None],
+    )
+    handed = pl.pallas_call(
         functools.partial(kernel, nspace),
         out_shape=(
-            jax.ShapeDtypeStruct((S, N), jnp.float32),
-            jax.ShapeDtypeStruct((1, N), jnp.float32),
+            pltpu.VMEM((6, R, CAP), jnp.float32),
+            pltpu.VMEM((2 * R, CELLS), jnp.bfloat16),
+            pltpu.VMEM((1, N), jnp.int32),
+            pltpu.VMEM((S, S), jnp.bfloat16),
+            pltpu.VMEM((S, 1), jnp.float32),
         ),
-        in_specs=[pl.BlockSpec(memory_space=pltpu.HBM)] * 9,
-        out_specs=(vmem, vmem),
+        in_specs=[hbm] * 9,
+        out_specs=(vmem,) * 5,
         scratch_shapes=[
             pltpu.VMEM((S, N), jnp.float32),
             pltpu.VMEM((1, N), jnp.float32),
@@ -299,7 +349,7 @@
             pltpu.VMEM((N, 128), jnp.int32),
             pltpu.VMEM((N, 128), jnp.int32),
             pltpu.VMEM((2, 5, R, CAP), jnp.float32),
-            pltpu.VMEM((2, 6, R, CAP), jnp.float32),
+            pltpu.VMEM((6, R, CAP), jnp.float32),
             pltpu.VMEM((2, R, CELLS), jnp.float32),
             pltpu.VMEM((2, R, CELLS), jnp.float32),
             pltpu.VMEM((2, 1, 256), jnp.float32),
@@ -312,19 +362,24 @@
             pltpu.SemaphoreType.DMA,
         ],
         compiler_params=pltpu.CompilerParams(
-            collective_id=0, has_side_effects=True, vmem_limit_bytes=67043328
+            collective_id=0, has_side_effects=True, vmem_limit_bytes=40 * 1024 * 1024
         ),
-    )(
-        species,
-        weight[None],
-        destination,
-        slot,
-        counts,
-        cell_index,
-        mix_rate[None],
-        rate_matrix,
-        rate_bias[None],
-    )
+    )(*(pltpu.with_memory_space_constraint(value, pltpu.HBM) for value in arguments))
+    out = pl.pallas_call(
+        finish,
+        out_shape=(
+            jax.ShapeDtypeStruct((S, N), jnp.float32),
+            jax.ShapeDtypeStruct((1, N), jnp.float32),
+        ),
+        in_specs=[vmem] * 5,
+        out_specs=(hbm, hbm),
+        scratch_shapes=[
+            pltpu.VMEM((S, N), jnp.float32),
+            pltpu.VMEM((1, N), jnp.float32),
+            pltpu.SemaphoreType.DMA((7,)),
+        ],
+        compiler_params=pltpu.CompilerParams(vmem_limit_bytes=40 * 1024 * 1024),
+    )(*(pltpu.with_memory_space_constraint(value, pltpu.VMEM) for value in handed))
     return out[0], out[1][0]
 
 

time: 47 us -> 43.2 us (0.919)
  local copies, waits for them, and re-layouts: 2.6 us -> 0 us
  Pallas kernels: 43.6 us -> 42.4 us
    unnamed x4 -> x0, local copies, waits for them, and re-layouts: 2.6 us -> none
    pallas_call x1 -> x2, Pallas kernels: 43.6 us -> 42.4 us  [the longest x1 40.6 us: shards(): pl.pallas_call(functools.partial(kernel, nspace), out_shape=(pltpu.VMEM((...]
where the time goes in v3:
time: 43.2 us; the launch traced here: 43.1 us
  Pallas kernels  42.4 us (98%)
  between operations  0.64 us (1%)
    pallas_call x1, Pallas kernels, shards(): pl.pallas_call(functools.partial(kernel, nspace), out_shape=(pltpu.VMEM((...  40.6 us
    pallas_call x1, Pallas kernels, shards(): pl.pallas_call(finish, out_shape=(jax.ShapeDtypeStruct((S, N), jnp.float3...  1.79 us

profile of v3, /device:TPU:1, one launch (start us, length us, event | category | flops | bytes accessed | tf_op | source)
XLA Modules:
  0.0 43.1 jit_solution(1042466377353314361)
XLA Ops:
  0.6 40.6 %shard_map.104 = (f32[6,56,512]{2,1,0:T(8,128)S(1)}, bf16[112,512]{1,0:T(8,128)(2,1)S(1)}, s32[1,3072]{1,0:T(1,128)S(1)}, bf16[54,54]{1,0:T(8,128)(2,1)S(1)}, f32[54,1]{1,0:T(8,128)S(1)}) custom-call(f32[54,3072]{1,0:T(8,128)} %species.1, f32[1,3072]{1,0:T(1,128)} %bitcast.4, s32[2,3072]{1,0:T(2,128)} %destination_in.1, s32[2,3072]{1,0:T(2,128)} %slot_in.1, ...), custom_call_target="tpu_custom_call" | custom-call | tf_op jit(solution)/shard_map/pallas_call | solution.py:327
  41.3 1.8 %shard_map.105 = (f32[54,3072]{1,0:T(8,128)}, f32[1,3072]{1,0:T(1,128)}) custom-call(f32[6,56,512]{2,1,0:T(8,128)S(1)} %get-tuple-element.9.landed, bf16[112,512]{1,0:T(8,128)(2,1)S(1)} %get-tuple-element.10.table_in, s32[1,3072]{1,0:T(1,128)S(1)} %get-tuple-element.11.cells_in, bf16[54,54]{1,0:T(8,128)(2,1)S(1)} %get-tuple-element.12.matrix_in, ...), custom_call_target="tpu_custom_call" | custom-call | tf_op jit(solution)/shard_map/pallas_call | solution.py:368

commit v4 on v3

--- a/solution.py
+++ b/solution.py
@@ -13,6 +13,7 @@
 N = 6 * CAP
 CELLS = 512
 KC = 256
+RELAYS = (28, 3)
 MESH = pl.DeviceIdType.MESH
 
 
@@ -120,6 +121,7 @@
     sums,
     sums_in,
     rates,
+    relay,
     load_sem,
     send_sem,
     recv_sem,
@@ -127,6 +129,8 @@
     sum_recv,
     rate_send,
     rate_recv,
+    relay_send,
+    relay_recv,
 ):
     slab = lax.axis_index("space")
     sub = lax.axis_index("sub")
@@ -137,9 +141,33 @@
     landed = (first_landed, last_landed)
 
     barrier = pltpu.get_barrier_semaphore()
-    peers = ((before, sub), (before, other), (after, sub), (after, other), (slab, other))
-    for peer in peers:
-        pl.semaphore_signal(barrier, inc=1, device_id=peer, device_id_type=MESH)
+    first, last = slab == 0, slab == nspace - 1
+    relays = jnp.logical_or(slab == RELAYS[0], slab == RELAYS[1])
+    relay_to = jnp.where(slab == RELAYS[0], sub, other)
+
+    def enter(*peers):
+        for peer in peers:
+            pl.semaphore_signal(barrier, inc=1, device_id=peer, device_id_type=MESH)
+
+    @pl.when(last)
+    def _():
+        enter((RELAYS[0], sub), (RELAYS[1], other))
+
+    @pl.when(jnp.logical_not(last))
+    def _():
+        enter((after, sub), (after, other))
+
+    enter((before, sub), (before, other), (slab, other))
+
+    @pl.when(first)
+    def _():
+        enter((RELAYS[0], sub), (RELAYS[1], sub))
+
+    @pl.when(relays)
+    def _():
+        enter((0, sub), (nspace - 1, relay_to))
+
+    entered = jnp.where(jnp.logical_or(last, relays), 7, 5)
     loads = []
     for source, target in (
         (destination_in, destination),
@@ -190,6 +218,38 @@
             device_id_type=MESH,
         )
         return 2 * kind + peer_sub, copy
+
+    def by_relay(send, device):
+        return pltpu.make_async_remote_copy(
+            src_ref=sending.at[0, send],
+            dst_ref=relay,
+            send_sem=send_sem.at[0, send],
+            recv_sem=relay_recv,
+            device_id=device,
+            device_id_type=MESH,
+        )
+
+    passed_on = pltpu.make_async_remote_copy(
+        src_ref=relay,
+        dst_ref=first_landed.at[4 + sub],
+        send_sem=relay_send,
+        recv_sem=recv_sem.at[0, 4 + sub],
+        device_id=(nspace - 1, relay_to),
+        device_id_type=MESH,
+    )
+
+    def start(step, i, copy):
+        if step == 0 and i in (1, 3):
+
+            @pl.when(first)
+            def _():
+                by_relay(i, (RELAYS[i // 2], sub)).start()
+
+            @pl.when(jnp.logical_not(first))
+            def _():
+                copy.start()
+        else:
+            copy.start()
 
     def arrived(step, land):
         pltpu.make_async_remote_copy(
@@ -251,8 +311,15 @@
             block, copy = sent(step, i)
             sending[step, i] = permuted(block)
             if step == 0 and i == 0:
-                pl.semaphore_wait(barrier, 5)
-            copy.start()
+                pl.semaphore_wait(barrier, entered)
+            start(step, i, copy)
+            if step == 0 and i == 0:
+
+                @pl.when(relays)
+                def _():
+                    by_relay(1, (slab, other)).wait_recv()
+                    passed_on.start()
+
             if step == 0 and i == 0:
                 rate_copy.start()
         landed[step][2 + sub] = permuted(2 + sub)
@@ -305,6 +372,10 @@
             last_table[...] = table
         for i in range(5):
             sent(step, i)[1].wait_send()
+
+    @pl.when(relays)
+    def _():
+        passed_on.wait_send()
 
 
 def shards(
@@ -353,11 +424,14 @@
             pltpu.VMEM((2, R, CELLS), jnp.float32),
             pltpu.VMEM((2, R, CELLS), jnp.float32),
             pltpu.VMEM((2, 1, 256), jnp.float32),
+            pltpu.VMEM((R, CAP), jnp.float32),
             pltpu.SemaphoreType.DMA((9,)),
             pltpu.SemaphoreType.DMA((2, 5)),
             pltpu.SemaphoreType.DMA((2, 6)),
             pltpu.SemaphoreType.DMA((2,)),
             pltpu.SemaphoreType.DMA((2,)),
+            pltpu.SemaphoreType.DMA,
+            pltpu.SemaphoreType.DMA,
             pltpu.SemaphoreType.DMA,
             pltpu.SemaphoreType.DMA,
         ],

time: 43.2 us -> 38 us (0.88)
  Pallas kernels: 42.4 us -> 37.2 us
    pallas_call x1, Pallas kernels: 40.6 us -> 35.4 us  [shards(): pl.pallas_call(functools.partial(kernel, nspace), out_shape=(pltpu.VMEM((...]
where the time goes in v4:
time: 38 us; the launch traced here: 37.9 us
  Pallas kernels  37.2 us (98%)
  between operations  0.64 us (2%)
    pallas_call x1, Pallas kernels, shards(): pl.pallas_call(functools.partial(kernel, nspace), out_shape=(pltpu.VMEM((...  35.4 us
    pallas_call x1, Pallas kernels, shards(): pl.pallas_call(finish, out_shape=(jax.ShapeDtypeStruct((S, N), jnp.float3...  1.79 us

profile of v4, /device:TPU:1, one launch (start us, length us, event | category | flops | bytes accessed | tf_op | source)
XLA Modules:
  0.0 37.9 jit_solution(9001604924554719421)
XLA Ops:
  0.6 35.4 %shard_map.104 = (f32[6,56,512]{2,1,0:T(8,128)S(1)}, bf16[112,512]{1,0:T(8,128)(2,1)S(1)}, s32[1,3072]{1,0:T(1,128)S(1)}, bf16[54,54]{1,0:T(8,128)(2,1)S(1)}, f32[54,1]{1,0:T(8,128)S(1)}) custom-call(f32[54,3072]{1,0:T(8,128)} %species.1, f32[1,3072]{1,0:T(1,128)} %bitcast.4, s32[2,3072]{1,0:T(2,128)} %destination_in.1, s32[2,3072]{1,0:T(2,128)} %slot_in.1, ...), custom_call_target="tpu_custom_call" | custom-call | tf_op jit(solution)/shard_map/pallas_call | solution.py:398
  36.1 1.8 %shard_map.105 = (f32[54,3072]{1,0:T(8,128)}, f32[1,3072]{1,0:T(1,128)}) custom-call(f32[6,56,512]{2,1,0:T(8,128)S(1)} %get-tuple-element.9.landed, bf16[112,512]{1,0:T(8,128)(2,1)S(1)} %get-tuple-element.10.table_in, s32[1,3072]{1,0:T(1,128)S(1)} %get-tuple-element.11.cells_in, bf16[54,54]{1,0:T(8,128)(2,1)S(1)} %get-tuple-element.12.matrix_in, ...), custom_call_target="tpu_custom_call" | custom-call | tf_op jit(solution)/shard_map/pallas_call | solution.py:442

commit v5 on v3

--- a/solution.py
+++ b/solution.py
@@ -13,6 +13,7 @@
 N = 6 * CAP
 CELLS = 512
 KC = 256
+RELAYS = (28, 3)
 MESH = pl.DeviceIdType.MESH
 
 
@@ -48,12 +49,12 @@
     return jnp.where(rows == jnp.broadcast_to(row, rows.shape), 1.0, 0.0).astype(jnp.bfloat16)
 
 
-def looked_up(table, cells, j):
+def looked_up(table, hot, j):
     total = jnp.zeros((2 * R, CAP), jnp.float32)
     for k in range(CELLS // KC):
         total = total + jnp.dot(
             table[:, k * KC : (k + 1) * KC],
-            hot_rows(cells[:, j * CAP : (j + 1) * CAP], k * KC, KC),
+            hot[k * KC : (k + 1) * KC, j * CAP : (j + 1) * CAP],
             preferred_element_type=jnp.float32,
         )
     return joined(total)
@@ -65,18 +66,18 @@
     return mixed + 0.5 * jnp.tanh(rate + bias)
 
 
-def finish(landed, table_in, cells_in, matrix_in, bias_in, species_out, weight_out, fresh, mass, sem):
+def finish(landed, table_in, hot, matrix_in, bias_in, species_out, weight_out, fresh, mass, sem):
     for j in range(6):
         mass[:, j * CAP : (j + 1) * CAP] = landed[j, S : S + 1, :]
     stores = [pltpu.make_async_copy(mass, weight_out, sem.at[6])]
     stores[0].start()
-    table, cells = table_in[...], cells_in[...]
+    table = table_in[...]
     matrix, bias = matrix_in[...], bias_in[...]
-    looked = looked_up(table, cells, 0)
+    looked = looked_up(table, hot, 0)
     for j in range(6):
         now = looked
         if j < 5:
-            looked = looked_up(table, cells, j + 1)
+            looked = looked_up(table, hot, j + 1)
         fresh[:, j * CAP : (j + 1) * CAP] = reacted(landed[j], now, matrix, bias)
         store = pltpu.make_async_copy(
             fresh.at[:, pl.ds(j * CAP, CAP)], species_out.at[:, pl.ds(j * CAP, CAP)], sem.at[j]
@@ -100,7 +101,7 @@
     bias_in,
     last_landed,
     last_table,
-    last_cells,
+    last_hot,
     matrix_out,
     bias_out,
     taken,
@@ -117,9 +118,11 @@
     cell_b,
     sending,
     first_landed,
+    first_hot,
     sums,
     sums_in,
     rates,
+    relay,
     load_sem,
     send_sem,
     recv_sem,
@@ -127,6 +130,8 @@
     sum_recv,
     rate_send,
     rate_recv,
+    relay_send,
+    relay_recv,
 ):
     slab = lax.axis_index("space")
     sub = lax.axis_index("sub")
@@ -137,9 +142,34 @@
     landed = (first_landed, last_landed)
 
     barrier = pltpu.get_barrier_semaphore()
-    peers = ((before, sub), (before, other), (after, sub), (after, other), (slab, other))
-    for peer in peers:
-        pl.semaphore_signal(barrier, inc=1, device_id=peer, device_id_type=MESH)
+    first, last = slab == 0, slab == nspace - 1
+    near, far = slab == RELAYS[0], slab == RELAYS[1]
+    relays = jnp.logical_or(near, far)
+    relay_to = jnp.where(near, sub, other)
+
+    def enter(*peers):
+        for peer in peers:
+            pl.semaphore_signal(barrier, inc=1, device_id=peer, device_id_type=MESH)
+
+    @pl.when(last)
+    def _():
+        enter((RELAYS[0], sub), (RELAYS[1], other))
+
+    @pl.when(jnp.logical_not(last))
+    def _():
+        enter((after, sub), (after, other))
+
+    enter((before, sub), (before, other), (slab, other))
+
+    @pl.when(first)
+    def _():
+        enter((RELAYS[0], 0), (RELAYS[0], 1), (RELAYS[1], sub))
+
+    @pl.when(relays)
+    def _():
+        enter((0, sub), (nspace - 1, relay_to))
+
+    entered = jnp.where(near, 8, jnp.where(jnp.logical_or(last, far), 7, 5))
     loads = []
     for source, target in (
         (destination_in, destination),
@@ -179,6 +209,8 @@
     def sent(step, i):
         kind = (2, 0, 2, 0, 1)[i]
         peer_sub = (sub, sub, other, other, other)[i]
+        if step == 1 and i in (0, 2):
+            peer_sub = jnp.where(last, 1 - peer_sub, peer_sub)
         peer_slab = (before, slab, after)[kind]
         land = 2 * (2 - kind) + sub
         copy = pltpu.make_async_remote_copy(
@@ -190,6 +222,64 @@
             device_id_type=MESH,
         )
         return 2 * kind + peer_sub, copy
+
+    def shared(ref, step):
+        return ref.at[:, pl.ds(0, CAP // 2)] if step else ref
+
+    def by_relay(step, i, device):
+        return pltpu.make_async_remote_copy(
+            src_ref=shared(sending.at[step, i], step),
+            dst_ref=shared(relay.at[step], step),
+            send_sem=send_sem.at[step, i],
+            recv_sem=relay_recv.at[step],
+            device_id=device,
+            device_id_type=MESH,
+        )
+
+    def passed_on(step):
+        land = sub if step else 4 + sub
+        return pltpu.make_async_remote_copy(
+            src_ref=shared(relay.at[step], step),
+            dst_ref=shared(landed[step].at[land], step),
+            send_sem=relay_send.at[step],
+            recv_sem=recv_sem.at[step, land],
+            device_id=(0, other) if step else (nspace - 1, relay_to),
+            device_id_type=MESH,
+        )
+
+    passing = (relays, near)
+
+    def pass_on(step):
+        @pl.when(passing[step])
+        def _():
+            by_relay(step, 0, (slab, other)).wait_recv()
+            passed_on(step).start()
+
+
+    def start(step, i, copy):
+        if (step, i) not in ((0, 1), (0, 3), (1, 0)):
+            copy.start()
+            return
+        detour = last if step else first
+
+        @pl.when(detour)
+        def _():
+            if step:
+                by_relay(1, i, (RELAYS[0], sub)).start()
+                pltpu.make_async_remote_copy(
+                    src_ref=sending.at[1, 0].at[:, pl.ds(CAP // 2, CAP // 2)],
+                    dst_ref=last_landed.at[sub].at[:, pl.ds(CAP // 2, CAP // 2)],
+                    send_sem=send_sem.at[1, 0],
+                    recv_sem=recv_sem.at[1, sub],
+                    device_id=(0, other),
+                    device_id_type=MESH,
+                ).start()
+            else:
+                by_relay(0, i, (RELAYS[i // 2], sub)).start()
+
+        @pl.when(jnp.logical_not(detour))
+        def _():
+            copy.start()
 
     def arrived(step, land):
         pltpu.make_async_remote_copy(
@@ -241,7 +331,6 @@
     rates[sub] = mix_rate[...]
     eye = lax.broadcasted_iota(jnp.int32, (S, S), 0) == lax.broadcasted_iota(jnp.int32, (S, S), 1)
     bias_column = jnp.sum(jnp.where(eye, bias[...], 0.0), axis=1, keepdims=True)
-    last_cells[...] = cell_index[1:2, :]
     matrix_out[...] = matrix[...]
     bias_out[...] = bias_column
     last_row = lax.broadcasted_iota(jnp.int32, (R, 1), 0) == S
@@ -251,10 +340,12 @@
             block, copy = sent(step, i)
             sending[step, i] = permuted(block)
             if step == 0 and i == 0:
-                pl.semaphore_wait(barrier, 5)
-            copy.start()
+                pl.semaphore_wait(barrier, entered)
+
+            start(step, i, copy)
             if step == 0 and i == 0:
                 rate_copy.start()
+                pass_on(0)
         landed[step][2 + sub] = permuted(2 + sub)
 
         cells = cell_index[step : step + 1, :]
@@ -263,11 +354,16 @@
             rate_copy.wait()
             column, live = routing(1)
             spread(column, col_b)
+        hot = (first_hot, last_hot)[step]
+        for k in range(CELLS // 64):
+            hot[k * 64 : (k + 1) * 64, :] = hot_rows(cells, k * 64, 64)
         decay = jnp.exp(-jnp.concatenate([rates[0], rates[1]], 1))
 
         total = jnp.zeros((2 * R, CELLS), jnp.float32)
         order = (2 + sub, 2 + other, sub, 4 + sub, other, 4 + other)
         for place, land in enumerate(order):
+            if step == 1 and place == 2:
+                pass_on(1)
             if place > 0:
                 arrived(step, land)
             value = landed[step][land]
@@ -280,6 +376,7 @@
                     hot_lanes(cell_b[rows, :], 0, CELLS),
                     preferred_element_type=jnp.float32,
                 )
+
         mine = joined(total)
         sums[step] = mine
         swap = exchange(step)
@@ -289,12 +386,12 @@
         mean = whole / jnp.maximum(whole[S : S + 1], 1.0)
         table = split(jnp.where(last_row, decay, mean * (1.0 - decay)))
         if step == 0:
-            looked = looked_up(table, cells, 0)
+            looked = looked_up(table, first_hot, 0)
             for j in range(6):
                 here = slice(j * CAP, (j + 1) * CAP)
                 now = looked
                 if j < 5:
-                    looked = looked_up(table, cells, j + 1)
+                    looked = looked_up(table, first_hot, j + 1)
                 value = first_landed[j]
                 fresh = reacted(value, now, matrix[...], bias_column)
                 mass = value[S : S + 1] * live[:, here]
@@ -305,6 +402,12 @@
             last_table[...] = table
         for i in range(5):
             sent(step, i)[1].wait_send()
+
+    for step in range(2):
+
+        @pl.when(passing[step])
+        def _():
+            passed_on(step).wait_send()
 
 
 def shards(
@@ -329,7 +432,7 @@
         out_shape=(
             pltpu.VMEM((6, R, CAP), jnp.float32),
             pltpu.VMEM((2 * R, CELLS), jnp.bfloat16),
-            pltpu.VMEM((1, N), jnp.int32),
+            pltpu.VMEM((CELLS, N), jnp.bfloat16),
             pltpu.VMEM((S, S), jnp.bfloat16),
             pltpu.VMEM((S, 1), jnp.float32),
         ),
@@ -350,9 +453,11 @@
             pltpu.VMEM((N, 128), jnp.int32),
             pltpu.VMEM((2, 5, R, CAP), jnp.float32),
             pltpu.VMEM((6, R, CAP), jnp.float32),
+            pltpu.VMEM((CELLS, N), jnp.bfloat16),
             pltpu.VMEM((2, R, CELLS), jnp.float32),
             pltpu.VMEM((2, R, CELLS), jnp.float32),
             pltpu.VMEM((2, 1, 256), jnp.float32),
+            pltpu.VMEM((2, R, CAP), jnp.float32),
             pltpu.SemaphoreType.DMA((9,)),
             pltpu.SemaphoreType.DMA((2, 5)),
             pltpu.SemaphoreType.DMA((2, 6)),
@@ -360,6 +465,8 @@
             pltpu.SemaphoreType.DMA((2,)),
             pltpu.SemaphoreType.DMA,
             pltpu.SemaphoreType.DMA,
+            pltpu.SemaphoreType.DMA((2,)),
+            pltpu.SemaphoreType.DMA((2,)),
         ],
         compiler_params=pltpu.CompilerParams(
             collective_id=0, has_side_effects=True, vmem_limit_bytes=40 * 1024 * 1024

time: 43.2 us -> 37.5 us (0.87)
  Pallas kernels: 42.4 us -> 36.7 us
    pallas_call x1, Pallas kernels: 40.6 us -> 35 us  [shards(): pl.pallas_call(functools.partial(kernel, nspace), out_shape=(pltpu.VMEM((...]
where the time goes in v5:
time: 37.5 us; the launch traced here: 37.4 us
  Pallas kernels  36.7 us (98%)
  between operations  0.64 us (2%)
    pallas_call x1, Pallas kernels, shards(): pl.pallas_call(functools.partial(kernel, nspace), out_shape=(pltpu.VMEM((...  35 us
    pallas_call x1, Pallas kernels, shards(): pl.pallas_call(finish, out_shape=(jax.ShapeDtypeStruct((S, N), jnp.float3...  1.74 us

profile of v5, /device:TPU:1, one launch (start us, length us, event | category | flops | bytes accessed | tf_op | source)
XLA Modules:
  0.0 37.4 jit_solution(6200647182075757884)
XLA Ops:
  0.6 35.0 %shard_map.104 = (f32[6,56,512]{2,1,0:T(8,128)S(1)}, bf16[112,512]{1,0:T(8,128)(2,1)S(1)}, bf16[512,3072]{1,0:T(8,128)(2,1)S(1)}, bf16[54,54]{1,0:T(8,128)(2,1)S(1)}, f32[54,1]{1,0:T(8,128)S(1)}) custom-call(f32[54,3072]{1,0:T(8,128)} %species.1, f32[1,3072]{1,0:T(1,128)} %bitcast.4, s32[2,3072]{1,0:T(2,128)} %destination_in.1, s32[2,3072]{1,0:T(2,128)} %slot_in.1, ...), custom_call_target="tpu_custom_call" | custom-call | tf_op jit(solution)/shard_map/pallas_call | solution.py:430
  35.6 1.7 %shard_map.105 = (f32[54,3072]{1,0:T(8,128)}, f32[1,3072]{1,0:T(1,128)}) custom-call(f32[6,56,512]{2,1,0:T(8,128)S(1)} %get-tuple-element.9.landed, bf16[112,512]{1,0:T(8,128)(2,1)S(1)} %get-tuple-element.10.table_in, bf16[512,3072]{1,0:T(8,128)(2,1)S(1)} %get-tuple-element.11.hot, bf16[54,54]{1,0:T(8,128)(2,1)S(1)} %get-tuple-element.12.matrix_in, ...), custom_call_target="tpu_custom_call" | custom-call | tf_op jit(solution)/shard_map/pallas_call | solution.py:475

commit v6 on v5

--- a/solution.py
+++ b/solution.py
@@ -310,12 +310,10 @@
             device_id_type=MESH,
         )
 
-    for load in loads[:3]:
+    for load in loads:
         load.wait()
     column, live = routing(0)
     spread(column, col_b)
-    for load in loads[3:]:
-        load.wait()
     for j in range(6):
         here = slice(j * CAP, (j + 1) * CAP)
         parts[:, here] = split(
@@ -400,10 +398,10 @@
                 )
         else:
             last_table[...] = table
+
+    for step in range(2):
         for i in range(5):
             sent(step, i)[1].wait_send()
-
-    for step in range(2):
 
         @pl.when(passing[step])
         def _():

time: 37.5 us -> 37.5 us (level)
  no operation moved by 1% of the time
where the time goes in v6:
time: 37.5 us; the launch traced here: 37.3 us
  Pallas kernels  36.7 us (98%)
  between operations  0.64 us (2%)
    pallas_call x1, Pallas kernels, shards(): pl.pallas_call(functools.partial(kernel, nspace), out_shape=(pltpu.VMEM((...  34.9 us
    pallas_call x1, Pallas kernels, shards(): pl.pallas_call(finish, out_shape=(jax.ShapeDtypeStruct((S, N), jnp.float3...  1.74 us

profile of v6, /device:TPU:1, one launch (start us, length us, event | category | flops | bytes accessed | tf_op | source)
XLA Modules:
  0.0 37.3 jit_solution(18396337252611503235)
XLA Ops:
  0.6 34.9 %shard_map.104 = (f32[6,56,512]{2,1,0:T(8,128)S(1)}, bf16[112,512]{1,0:T(8,128)(2,1)S(1)}, bf16[512,3072]{1,0:T(8,128)(2,1)S(1)}, bf16[54,54]{1,0:T(8,128)(2,1)S(1)}, f32[54,1]{1,0:T(8,128)S(1)}) custom-call(f32[54,3072]{1,0:T(8,128)} %species.1, f32[1,3072]{1,0:T(1,128)} %bitcast.4, s32[2,3072]{1,0:T(2,128)} %destination_in.1, s32[2,3072]{1,0:T(2,128)} %slot_in.1, ...), custom_call_target="tpu_custom_call" | custom-call | tf_op jit(solution)/shard_map/pallas_call | solution.py:428
  35.6 1.7 %shard_map.105 = (f32[54,3072]{1,0:T(8,128)}, f32[1,3072]{1,0:T(1,128)}) custom-call(f32[6,56,512]{2,1,0:T(8,128)S(1)} %get-tuple-element.9.landed, bf16[112,512]{1,0:T(8,128)(2,1)S(1)} %get-tuple-element.10.table_in, bf16[512,3072]{1,0:T(8,128)(2,1)S(1)} %get-tuple-element.11.hot, bf16[54,54]{1,0:T(8,128)(2,1)S(1)} %get-tuple-element.12.matrix_in, ...), custom_call_target="tpu_custom_call" | custom-call | tf_op jit(solution)/shard_map/pallas_call | solution.py:473

commit v7 on v6

--- a/solution.py
+++ b/solution.py
@@ -224,7 +224,7 @@
         return 2 * kind + peer_sub, copy
 
     def shared(ref, step):
-        return ref.at[:, pl.ds(0, CAP // 2)] if step else ref
+        return ref.at[:, pl.ds(0, CAP // 4)] if step else ref
 
     def by_relay(step, i, device):
         return pltpu.make_async_remote_copy(
@@ -267,8 +267,8 @@
             if step:
                 by_relay(1, i, (RELAYS[0], sub)).start()
                 pltpu.make_async_remote_copy(
-                    src_ref=sending.at[1, 0].at[:, pl.ds(CAP // 2, CAP // 2)],
-                    dst_ref=last_landed.at[sub].at[:, pl.ds(CAP // 2, CAP // 2)],
+                    src_ref=sending.at[1, 0].at[:, pl.ds(CAP // 4, CAP - CAP // 4)],
+                    dst_ref=last_landed.at[sub].at[:, pl.ds(CAP // 4, CAP - CAP // 4)],
                     send_sem=send_sem.at[1, 0],
                     recv_sem=recv_sem.at[1, sub],
                     device_id=(0, other),

time: 37.5 us -> 38 us (1.013)
  Pallas kernels: 36.7 us -> 37.3 us
    pallas_call x1, Pallas kernels: 34.9 us -> 35.5 us  [shards(): pl.pallas_call(functools.partial(kernel, nspace), out_shape=(pltpu.VMEM((...]
where the time goes in v7:
time: 38 us; the launch traced here: 37.9 us
  Pallas kernels  37.3 us (98%)
  between operations  0.64 us (2%)
    pallas_call x1, Pallas kernels, shards(): pl.pallas_call(functools.partial(kernel, nspace), out_shape=(pltpu.VMEM((...  35.5 us
    pallas_call x1, Pallas kernels, shards(): pl.pallas_call(finish, out_shape=(jax.ShapeDtypeStruct((S, N), jnp.float3...  1.75 us

profile of v7, /device:TPU:1, one launch (start us, length us, event | category | flops | bytes accessed | tf_op | source)
XLA Modules:
  0.0 37.9 jit_solution(3762930445607364914)
XLA Ops:
  0.6 35.5 %shard_map.104 = (f32[6,56,512]{2,1,0:T(8,128)S(1)}, bf16[112,512]{1,0:T(8,128)(2,1)S(1)}, bf16[512,3072]{1,0:T(8,128)(2,1)S(1)}, bf16[54,54]{1,0:T(8,128)(2,1)S(1)}, f32[54,1]{1,0:T(8,128)S(1)}) custom-call(f32[54,3072]{1,0:T(8,128)} %species.1, f32[1,3072]{1,0:T(1,128)} %bitcast.4, s32[2,3072]{1,0:T(2,128)} %destination_in.1, s32[2,3072]{1,0:T(2,128)} %slot_in.1, ...), custom_call_target="tpu_custom_call" | custom-call | tf_op jit(solution)/shard_map/pallas_call | solution.py:428
  36.2 1.7 %shard_map.105 = (f32[54,3072]{1,0:T(8,128)}, f32[1,3072]{1,0:T(1,128)}) custom-call(f32[6,56,512]{2,1,0:T(8,128)S(1)} %get-tuple-element.9.landed, bf16[112,512]{1,0:T(8,128)(2,1)S(1)} %get-tuple-element.10.table_in, bf16[512,3072]{1,0:T(8,128)(2,1)S(1)} %get-tuple-element.11.hot, bf16[54,54]{1,0:T(8,128)(2,1)S(1)} %get-tuple-element.12.matrix_in, ...), custom_call_target="tpu_custom_call" | custom-call | tf_op jit(solution)/shard_map/pallas_call | solution.py:473
